TPU v7x, 256 devices: a whole 4x4x8 slice. The times are simulated.
256 devices in a mesh: space: 16 (over x, z_hi), tm: 16 (over y, z_lo, core).
Axes of the slice: x: 4, y: 4, z: 8 (z_hi: 4, z_lo: 2; z = z_hi * 2 + z_lo), core: 2. Of those that a mesh axis runs over, the one named last changes fastest.
Arguments:
- latent: float32 [24, 1024, 2048], P(None, 'space', 'tm'), may hold values from -1.8 to 1.8
- events: int32 [24, 1024, 2048], P(None, 'space', 'tm'), may hold values from 0 to 7
- log_base: float32 [24, 1024, 2048], P(None, 'space', 'tm'), may hold values from -1.5 to 0.5
- innovation: float32 [24, 1024, 2048], P(None, 'space', 'tm'), may hold values from -6 to 6
- kappa_sq: float32 [24, 1024], replicated, may hold values from 0.3 to 3
- chol_factor: float32 [2048, 2048], P(None, 'tm'), as said below
- step_size: float32 [1], replicated, may hold values from 0.02 to 0.08
Outputs:
- gradient: float32 [24, 1024, 2048], P(None, 'space', 'tm')
- proposal: float32 [24, 1024, 2048], P(None, 'space', 'tm')
Inputs may be any that keep to these rules, and one draw needn't show every extreme that they name: chol_factor is lower triangular with a positive diagonal.
All inputs are finite; a program needn't handle non-finite values.
Results may differ from a plain program's by a relative error of at most 0.000067.
Values sent between devices are 32-bit elements; how exact they have to be, the bound alone decides.
A program may use at most 64 MiB of HBM per device.

v0:
```python
import jax
import jax.numpy as jnp
from jax import lax
from jax.sharding import PartitionSpec as P


def padded(block, sides, width):
    for axis, dim in sides:
        count = lax.axis_size(axis)
        forward = [(i, i + 1) for i in range(count - 1)]
        backward = [(target, source) for source, target in forward]
        low = lax.ppermute(
            lax.slice_in_dim(block, block.shape[dim] - width, None, axis=dim), axis, forward
        )
        high = lax.ppermute(lax.slice_in_dim(block, 0, width, axis=dim), axis, backward)
        block = jnp.concatenate([low, block, high], axis=dim)
    return block


def operate(extended, kappa_cols):
    centre = extended[:, 1:-1]
    row_padded = jnp.pad(centre, ((1, 1), (0, 0), (0, 0)))
    beside = row_padded[2:] + row_padded[:-2]
    beside = beside + extended[:, 2:] + extended[:, :-2]
    return (kappa_cols[:, :, None] + 4.0) * centre - beside


def face_halo(field):
    return padded(field, (("space", 1),), 1)


def local(latent, events, log_base, innovation, kappa_sq, chol_factor, step_size):
    row_count, col_count, time_count = latent.shape
    col_index = lax.axis_index("space")
    padded_kappa = jnp.pad(kappa_sq, ((0, 0), (2, 2)))
    first_col = col_index * col_count + 2 - 0
    kappa_here = lax.dynamic_slice(
        padded_kappa, (jnp.int32(0), first_col), (row_count, col_count + 2 * 0)
    )
    first_pass = operate(face_halo(latent), kappa_here)
    spatial = operate(face_halo(first_pass), kappa_here)
    cell_count = row_count * col_count
    flattened = spatial.reshape(cell_count, time_count)
    factor_rows = chol_factor
    projected = jnp.dot(
        lax.all_gather(flattened, "tm", axis=1, tiled=True),
        factor_rows,
        precision=lax.Precision.HIGHEST,
        preferred_element_type=jnp.float32,
    )
    factor_rows = chol_factor
    by_hour = lax.psum_scatter(
        lax.dot_general(
            factor_rows,
            projected,
            (((1,), (1,)), ((), ())),
            precision=lax.Precision.HIGHEST,
            preferred_element_type=jnp.float32,
        ),
        "tm",
        scatter_dimension=0,
        tiled=True,
    )
    prior_term = by_hour.T.reshape(row_count, col_count, time_count)
    gradient = events.astype(jnp.float32) - jnp.exp(log_base + latent) - prior_term
    proposal = latent + step_size[0] * gradient + jnp.sqrt(2.0 * step_size[0]) * innovation
    return (gradient, proposal)


def solution(mesh):
    in_specs = (
        P(None, "space", "tm"),
        P(None, "space", "tm"),
        P(None, "space", "tm"),
        P(None, "space", "tm"),
        P(),
        P(None, "tm"),
        P(),
    )
    out_specs = (P(None, "space", "tm"), P(None, "space", "tm"))
    return jax.shard_map(local, mesh=mesh, in_specs=in_specs, out_specs=out_specs, check_vma=False)
```

profile of v0, /device:TPU:2, one launch (start us, length us, event | category | flops | bytes accessed | tf_op | source)
XLA Modules:
  0.0 296.3 jit_solution(11682274919811678598)
XLA Ops:
  7.2 0.0 copy-start
  7.2 0.0 all-gather.2.cloned.1.call-start
  7.2 1.0 fusion.10
  8.3 8.2 %collective-permute-start = (f32[24,1,128]{2,1,0:T(1,128)S(1)}, f32[24,1,128]{2,1,0:T(1,128)S(1)}, u32[]{:S(2)}, u32[]{:S(2)}) collective-permute-start(f32[24,1,128]{2,1,0:T(1,128)S(1)} %get-tuple-element.6), channel_id=1, source_target_pairs={{16,0},{32,16},{48,32},{64,48},{80,64},{96,80},{112,96},{128,112},... | collective-permute-start | bytes 36872 | tf_op jit(solution)/shard_map/ppermute | solution.py:15
  16.5 1.9 collective-permute-start.1
  18.4 0.9 fusion.8
  19.2 0.0 collective-permute-done
  19.2 5.8 %collective-permute-done.1 = f32[24,1,128]{2,1,0:T(1,128)S(1)} collective-permute-done((f32[24,1,128]{2,1,0:T(1,128)S(1)}, f32[24,1,128]{2,1,0:T(1,128)S(1)}, u32[]{:S(2)}, u32[]{:S(2)}) %collective-permute-start.1) | collective-permute-done | bytes 12320 | tf_op jit(solution)/shard_map/ppermute | solution.py:12
  25.1 2.9 fusion.3
  28.0 1.9 collective-permute-start.2
  29.9 4.8 %collective-permute-start.3 = (f32[24,1,128]{2,1,0:T(1,128)S(1)}, f32[24,1,128]{2,1,0:T(1,128)S(1)}, u32[]{:S(2)}, u32[]{:S(2)}) collective-permute-start(f32[24,1,128]{2,1,0:T(1,128)S(1)} %get-tuple-element.5), channel_id=1, source_target_pairs={{0,16},{16,32},{32,48},{48,64},{64,80},{80,96},{96,112},{112,128},... | collective-permute-start | bytes 36872 | tf_op jit(solution)/shard_map/ppermute | solution.py:12
  34.7 0.0 collective-permute-done.2
  34.7 3.8 %collective-permute-done.3 = f32[24,1,128]{2,1,0:T(1,128)S(1)} collective-permute-done((f32[24,1,128]{2,1,0:T(1,128)S(1)}, f32[24,1,128]{2,1,0:T(1,128)S(1)}, u32[]{:S(2)}, u32[]{:S(2)}) %collective-permute-start.3) | collective-permute-done | bytes 12320 | tf_op jit(solution)/shard_map/ppermute | solution.py:12
  38.5 1.2 fusion.7
  39.7 0.0 all-gather.2.cloned.1.call-update
  39.7 0.0 reduce-scatter.2.cloned.1.call-start
  39.8 79.2 %all-gather.2.cloned.1.call-done = f32[1536,2048]{1,0:T(8,128)} async-done(((f32[1536,128]{1,0:T(8,128)}), f32[1536,2048]{1,0:T(8,128)}) %all-gather.2.cloned.1.call-update) | async-done | bytes 12582928 | tf_op jit(solution)/shard_map/all_gather | solution.py:46
  119.0 0.0 copy-done
  119.0 12.5 %fusion.11 = f32[1536,128]{1,0:T(8,128)S(1)} fusion(f32[1536,2048]{1,0:T(8,128)} %all-gather.2.cloned.1.call-done, f32[2048,128]{1,0:T(8,128)S(1)} %copy-done), kind=kOutput, calls=%fused_computation.23 | convolution fusion | flops 4831838208 | bytes 14417920 | tf_op jit(solution)/shard_map/dot_general | solution.py:45
  131.5 0.0 copy-start.1
  131.5 0.0 copy-start.2
  131.5 0.0 copy-start.3
  131.5 12.3 %convolution_bitcast_fusion = f32[2048,1536]{0,1:T(8,128)} fusion(f32[1536,128]{1,0:T(8,128)S(1)} %fusion.11, f32[2048,128]{1,0:T(8,128)S(1)} %copy-done), kind=kOutput, calls=%fused_computation | convolution fusion | flops 4831838208 | bytes 14417920 | tf_op jit(solution)/shard_map/dot_general | solution.py:53
  143.8 0.0 reduce-scatter.2.cloned.1.call-update
  144.5 142.1 %reduce-scatter.2.cloned.1.call-done = f32[128,1536]{0,1:T(8,128)} async-done(((f32[2048,1536]{0,1:T(8,128)}), f32[128,1536]{0,1:T(8,128)}) %reduce-scatter.2.cloned.1.call-update) | async-done | bytes 786448 | tf_op jit(solution)/shard_map/reduce_scatter | solution.py:52
  286.6 0.0 copy-done.1
  286.6 0.0 copy-done.2
  286.6 0.0 copy-done.3
  286.6 2.9 multiply_add_fusion
  (1 shorter events, 0.0 us)
Async XLA Ops:
  7.2 111.8 %copy-start = (f32[2048,128]{1,0:T(8,128)S(1)}, f32[2048,128]{1,0:T(8,128)}, u32[]{:S(2)}) copy-start(f32[2048,128]{1,0:T(8,128)} %param.12) | copy-start | bytes 3145732
  7.2 111.8 %all-gather.2.cloned.1.call-start = ((), (), s32[]{:S(2)}) async-start(), calls=%async_computation.1 | async-start | bytes 13369344 | tf_op jit(solution)/shard_map/all_gather | solution.py:46
  8.3 11.0 %collective-permute-start = (f32[24,1,128]{2,1,0:T(1,128)S(1)}, f32[24,1,128]{2,1,0:T(1,128)S(1)}, u32[]{:S(2)}, u32[]{:S(2)}) collective-permute-start(f32[24,1,128]{2,1,0:T(1,128)S(1)} %get-tuple-element.6), channel_id=1, source_target_pairs={{16,0},{32,16},{48,32},{64,48},{80,64},{96,80},{112,96},{128,112},... | collective-permute-start | bytes 36872 | tf_op jit(solution)/shard_map/ppermute | solution.py:15
  16.5 8.6 %collective-permute-start.1 = (f32[24,1,128]{2,1,0:T(1,128)S(1)}, f32[24,1,128]{2,1,0:T(1,128)S(1)}, u32[]{:S(2)}, u32[]{:S(2)}) collective-permute-start(f32[24,1,128]{2,1,0:T(1,128)S(1)} %get-tuple-element.7), channel_id=1, source_target_pairs={{0,16},{16,32},{32,48},{48,64},{64,80},{80,96},{96,112},{112,128},... | collective-permute-start | bytes 36872 | tf_op jit(solution)/shard_map/ppermute | solution.py:12
  28.0 6.8 %collective-permute-start.2 = (f32[24,1,128]{2,1,0:T(1,128)S(1)}, f32[24,1,128]{2,1,0:T(1,128)S(1)}, u32[]{:S(2)}, u32[]{:S(2)}) collective-permute-start(f32[24,1,128]{2,1,0:T(1,128)S(1)} %get-tuple-element.4), channel_id=1, source_target_pairs={{16,0},{32,16},{48,32},{64,48},{80,64},{96,80},{112,96},{128,112},... | collective-permute-start | bytes 36872 | tf_op jit(solution)/shard_map/ppermute | solution.py:15
  29.9 8.6 %collective-permute-start.3 = (f32[24,1,128]{2,1,0:T(1,128)S(1)}, f32[24,1,128]{2,1,0:T(1,128)S(1)}, u32[]{:S(2)}, u32[]{:S(2)}) collective-permute-start(f32[24,1,128]{2,1,0:T(1,128)S(1)} %get-tuple-element.5), channel_id=1, source_target_pairs={{0,16},{16,32},{32,48},{48,64},{64,80},{80,96},{96,112},{112,128},... | collective-permute-start | bytes 36872 | tf_op jit(solution)/shard_map/ppermute | solution.py:12
  39.7 246.9 %reduce-scatter.2.cloned.1.call-start = ((), (), s32[]{:S(2)}) async-start(), calls=%async_computation.2 | async-start | bytes 13369344 | tf_op jit(solution)/shard_map/reduce_scatter | solution.py:52
  131.5 155.1 %copy-start.1 = (f32[24,64,128]{2,1,0:T(8,128)S(1)}, f32[24,64,128]{2,1,0:T(8,128)}, u32[]{:S(2)}) copy-start(f32[24,64,128]{2,1,0:T(8,128)} %param.7) | copy-start | bytes 2359300
  131.5 155.1 %copy-start.2 = (f32[24,64,128]{2,1,0:T(8,128)S(1)}, f32[24,64,128]{2,1,0:T(8,128)}, u32[]{:S(2)}) copy-start(f32[24,64,128]{2,1,0:T(8,128)} %param.10) | copy-start | bytes 2359300
  131.5 155.1 %copy-start.3 = (f32[24,64,128]{2,1,0:T(8,128)S(1)}, f32[24,64,128]{2,1,0:T(8,128)}, u32[]{:S(2)}) copy-start(f32[24,64,128]{2,1,0:T(8,128)} %param.9) | copy-start | bytes 2359300
Sparse Core Ops, SparseCore 0:
  39.8 79.1 all-gather.1
  143.9 142.5 reduce-scatter.1
where the time goes:
time: 297 us; the launch traced here: 296 us
  waiting for transfers between devices  231 us (78%)
  matrix products  24.8 us (8%)
  starting transfers between devices  16.9 us (6%)
  between operations  14.8 us (5%)
  other arithmetic  7.85 us (3%)
    reduce_scatter x1, waiting for transfers between devices, local(): lax.psum_scatter(lax.dot_general(factor_rows, projected, (((1,), (1,)), (...  142 us
    all_gather x1, waiting for transfers between devices, local(): lax.all_gather(flattened, 'tm', axis=1, tiled=True)  79.2 us
    dot_general x1, matrix products, local(): jnp.dot(lax.all_gather(flattened, 'tm', axis=1, tiled=True), factor_rows,...  12.5 us
    dot_general x1, matrix products, local(): lax.dot_general(factor_rows, projected, (((1,), (1,)), ((), ())), precisi...  12.3 us
    ppermute x2, starting transfers between devices, padded(): lax.ppermute(lax.slice_in_dim(block, 0, width, axis=dim), axis, backward)  10.1 us
    ppermute x2, waiting for transfers between devices, padded(): lax.ppermute(lax.slice_in_dim(block, block.shape[dim] - width, None, axis...  9.56 us
    ppermute x2, starting transfers between devices, padded(): lax.ppermute(lax.slice_in_dim(block, block.shape[dim] - width, None, axis...  6.74 us
  transfers between devices with their start and end apart: 6, of which 4 were waited for; matrix products, arithmetic and copies ran while one was open for 0% of the time, Pallas kernels for 0%

commit v1 on v0

--- a/solution.py
+++ b/solution.py
@@ -43,7 +43,9 @@
     flattened = spatial.reshape(cell_count, time_count)
     factor_rows = chol_factor
     projected = jnp.dot(
-        lax.all_gather(flattened, "tm", axis=1, tiled=True),
+        jnp.concatenate(
+            lax.all_to_all(jnp.stack([flattened] * lax.axis_size("tm")), "tm", 0, 0), axis=1
+        ),
         factor_rows,
         precision=lax.Precision.HIGHEST,
         preferred_element_type=jnp.float32,

time: 297 us -> 366 us (1.23)
  blocking collectives: 0 us -> 145 us
  waiting for transfers between devices: 231 us -> 147 us
  matrix products: 24.8 us -> 33.1 us
    all_to_all x0 -> x1, blocking collectives: none -> 145 us  [local(): lax.all_to_all(jnp.stack([flattened] * lax.axis_size('tm')), 'tm', 0, 0)]
    all_gather x1 -> x0, waiting for transfers between devices: 79.2 us -> none  [local(): lax.all_gather(flattened, 'tm', axis=1, tiled=True)]
    dot_general x1, matrix products: 12.5 us -> 20.8 us  [local(): jnp.dot(jnp.concatenate(lax.all_to_all(jnp.stack([flattened] * lax.axis_s...]
    reduce_scatter x1, waiting for transfers between devices: 142 us -> 137 us  [local(): lax.psum_scatter(lax.dot_general(factor_rows, projected, (((1,), (1,)), (...]
  transfers between devices with their start and end apart: 6 -> 5, of which waited for: 4 -> 3; matrix products, arithmetic and copies ran while one was open for 0% -> 0% of each run, Pallas kernels for 0% -> 0%
where the time goes in v1:
time: 366 us
  waiting for transfers between devices  147 us (40%)
  blocking collectives  145 us (40%)
  matrix products  33.1 us (9%)
  starting transfers between devices  16.9 us (5%)
  between operations  14.8 us (4%)
  other arithmetic  6.8 us (2%)
    all_to_all x1, blocking collectives, local(): lax.all_to_all(jnp.stack([flattened] * lax.axis_size('tm')), 'tm', 0, 0)  145 us
    reduce_scatter x1, waiting for transfers between devices, local(): lax.psum_scatter(lax.dot_general(factor_rows, projected, (((1,), (1,)), (...  137 us
    dot_general x1, matrix products, local(): jnp.dot(jnp.concatenate(lax.all_to_all(jnp.stack([flattened] * lax.axis_s...  20.8 us
    dot_general x1, matrix products, local(): lax.dot_general(factor_rows, projected, (((1,), (1,)), ((), ())), precisi...  12.3 us
    ppermute x2, starting transfers between devices, padded(): lax.ppermute(lax.slice_in_dim(block, 0, width, axis=dim), axis, backward)  10.1 us
    ppermute x2, waiting for transfers between devices, padded(): lax.ppermute(lax.slice_in_dim(block, block.shape[dim] - width, None, axis...  9.56 us
  transfers between devices with their start and end apart: 5, of which 3 were waited for; matrix products, arithmetic and copies ran while one was open for 0% of the time, Pallas kernels for 0%

profile of v1, /device:TPU:2, one launch (start us, length us, event | category | flops | bytes accessed | tf_op | source)
XLA Modules:
  0.0 366.1 jit_solution(8558825349638186980)
XLA Ops:
  7.2 0.0 copy-start
  7.2 0.0 reduce-scatter.2.cloned.1.call-start
  7.2 1.0 fusion.10
  8.3 8.2 %collective-permute-start = (f32[24,1,128]{2,1,0:T(1,128)S(1)}, f32[24,1,128]{2,1,0:T(1,128)S(1)}, u32[]{:S(2)}, u32[]{:S(2)}) collective-permute-start(f32[24,1,128]{2,1,0:T(1,128)S(1)} %get-tuple-element.6), channel_id=1, source_target_pairs={{16,0},{32,16},{48,32},{64,48},{80,64},{96,80},{112,96},{128,112},... | collective-permute-start | bytes 36872 | tf_op jit(solution)/shard_map/ppermute | solution.py:15
  16.5 1.9 collective-permute-start.1
  18.4 0.9 fusion.8
  19.2 0.0 collective-permute-done
  19.2 5.8 %collective-permute-done.1 = f32[24,1,128]{2,1,0:T(1,128)S(1)} collective-permute-done((f32[24,1,128]{2,1,0:T(1,128)S(1)}, f32[24,1,128]{2,1,0:T(1,128)S(1)}, u32[]{:S(2)}, u32[]{:S(2)}) %collective-permute-start.1) | collective-permute-done | bytes 12320 | tf_op jit(solution)/shard_map/ppermute | solution.py:12
  25.1 2.7 fusion.3
  27.8 1.9 collective-permute-start.2
  29.7 4.8 %collective-permute-start.3 = (f32[24,1,128]{2,1,0:T(1,128)S(1)}, f32[24,1,128]{2,1,0:T(1,128)S(1)}, u32[]{:S(2)}, u32[]{:S(2)}) collective-permute-start(f32[24,1,128]{2,1,0:T(1,128)S(1)} %get-tuple-element.5), channel_id=1, source_target_pairs={{0,16},{16,32},{32,48},{48,64},{64,80},{80,96},{96,112},{112,128},... | collective-permute-start | bytes 36872 | tf_op jit(solution)/shard_map/ppermute | solution.py:12
  34.5 0.0 collective-permute-done.2
  34.5 3.8 %collective-permute-done.3 = f32[24,1,128]{2,1,0:T(1,128)S(1)} collective-permute-done((f32[24,1,128]{2,1,0:T(1,128)S(1)}, f32[24,1,128]{2,1,0:T(1,128)S(1)}, u32[]{:S(2)}, u32[]{:S(2)}) %collective-permute-start.3) | collective-permute-done | bytes 12320 | tf_op jit(solution)/shard_map/ppermute | solution.py:12
  38.3 0.3 fusion.7
  38.6 0.3 copy.9
  38.9 1.6 stack.3
  40.5 144.9 %all_to_all.5 = f32[16,1536,128]{1,2,0:T(8,128)S(1)} all-to-all(f32[16,1536,128]{1,2,0:T(8,128)S(1)} %stack.3), channel_id=1, replica_groups=mesh['space'=16,'tm'=16] {'tm'}, dimensions={0} | all-to-all | bytes 25165824 | tf_op jit(solution)/shard_map/all_to_all | solution.py:47
  185.4 0.0 copy-done
  185.4 20.8 %fusion.11 = f32[1536,128]{1,0:T(8,128)S(1)} fusion(f32[1536,2048]{0,1:T(8,128)S(1)} %bitcast.16, f32[2048,128]{1,0:T(8,128)S(1)} %copy-done), kind=kOutput, calls=%fused_computation.23 | convolution fusion | flops 4831838208 | bytes 14417920 | tf_op jit(solution)/shard_map/dot_general | solution.py:45
  206.2 0.0 copy-start.1
  206.2 0.0 copy-start.2
  206.2 0.0 copy-start.3
  206.2 12.3 %convolution_bitcast_fusion = f32[2048,1536]{0,1:T(8,128)} fusion(f32[1536,128]{1,0:T(8,128)S(1)} %fusion.11, f32[2048,128]{1,0:T(8,128)S(1)} %copy-done), kind=kOutput, calls=%fused_computation | convolution fusion | flops 4831838208 | bytes 14417920 | tf_op jit(solution)/shard_map/dot_general | solution.py:55
  218.5 0.0 reduce-scatter.2.cloned.1.call-update
  219.2 137.1 %reduce-scatter.2.cloned.1.call-done = f32[128,1536]{0,1:T(8,128)} async-done(((f32[2048,1536]{0,1:T(8,128)}), f32[128,1536]{0,1:T(8,128)}) %reduce-scatter.2.cloned.1.call-update) | async-done | bytes 786448 | tf_op jit(solution)/shard_map/reduce_scatter | solution.py:54
  356.3 0.0 copy-done.1
  356.3 0.0 copy-done.2
  356.3 0.0 copy-done.3
  356.3 2.9 multiply_add_fusion
  (1 shorter events, 0.0 us)
Async XLA Ops:
  7.2 178.2 %copy-start = (f32[2048,128]{1,0:T(8,128)S(1)}, f32[2048,128]{1,0:T(8,128)}, u32[]{:S(2)}) copy-start(f32[2048,128]{1,0:T(8,128)} %param.12) | copy-start | bytes 3145732
  7.2 349.1 %reduce-scatter.2.cloned.1.call-start = ((), (), s32[]{:S(2)}) async-start(), calls=%async_computation.2 | async-start | bytes 13369344 | tf_op jit(solution)/shard_map/reduce_scatter | solution.py:54
  8.3 11.0 %collective-permute-start = (f32[24,1,128]{2,1,0:T(1,128)S(1)}, f32[24,1,128]{2,1,0:T(1,128)S(1)}, u32[]{:S(2)}, u32[]{:S(2)}) collective-permute-start(f32[24,1,128]{2,1,0:T(1,128)S(1)} %get-tuple-element.6), channel_id=1, source_target_pairs={{16,0},{32,16},{48,32},{64,48},{80,64},{96,80},{112,96},{128,112},... | collective-permute-start | bytes 36872 | tf_op jit(solution)/shard_map/ppermute | solution.py:15
  16.5 8.6 %collective-permute-start.1 = (f32[24,1,128]{2,1,0:T(1,128)S(1)}, f32[24,1,128]{2,1,0:T(1,128)S(1)}, u32[]{:S(2)}, u32[]{:S(2)}) collective-permute-start(f32[24,1,128]{2,1,0:T(1,128)S(1)} %get-tuple-element.7), channel_id=1, source_target_pairs={{0,16},{16,32},{32,48},{48,64},{64,80},{80,96},{96,112},{112,128},... | collective-permute-start | bytes 36872 | tf_op jit(solution)/shard_map/ppermute | solution.py:12
  27.8 6.8 %collective-permute-start.2 = (f32[24,1,128]{2,1,0:T(1,128)S(1)}, f32[24,1,128]{2,1,0:T(1,128)S(1)}, u32[]{:S(2)}, u32[]{:S(2)}) collective-permute-start(f32[24,1,128]{2,1,0:T(1,128)S(1)} %get-tuple-element.4), channel_id=1, source_target_pairs={{16,0},{32,16},{48,32},{64,48},{80,64},{96,80},{112,96},{128,112},... | collective-permute-start | bytes 36872 | tf_op jit(solution)/shard_map/ppermute | solution.py:15
  29.7 8.6 %collective-permute-start.3 = (f32[24,1,128]{2,1,0:T(1,128)S(1)}, f32[24,1,128]{2,1,0:T(1,128)S(1)}, u32[]{:S(2)}, u32[]{:S(2)}) collective-permute-start(f32[24,1,128]{2,1,0:T(1,128)S(1)} %get-tuple-element.5), channel_id=1, source_target_pairs={{0,16},{16,32},{32,48},{48,64},{64,80},{80,96},{96,112},{112,128},... | collective-permute-start | bytes 36872 | tf_op jit(solution)/shard_map/ppermute | solution.py:12
  206.2 150.1 %copy-start.1 = (f32[24,64,128]{2,1,0:T(8,128)S(1)}, f32[24,64,128]{2,1,0:T(8,128)}, u32[]{:S(2)}) copy-start(f32[24,64,128]{2,1,0:T(8,128)} %param.7) | copy-start | bytes 2359300
  206.2 150.1 %copy-start.2 = (f32[24,64,128]{2,1,0:T(8,128)S(1)}, f32[24,64,128]{2,1,0:T(8,128)}, u32[]{:S(2)}) copy-start(f32[24,64,128]{2,1,0:T(8,128)} %param.10) | copy-start | bytes 2359300
  206.2 150.1 %copy-start.3 = (f32[24,64,128]{2,1,0:T(8,128)S(1)}, f32[24,64,128]{2,1,0:T(8,128)}, u32[]{:S(2)}) copy-start(f32[24,64,128]{2,1,0:T(8,128)} %param.9) | copy-start | bytes 2359300
Sparse Core Ops, SparseCore 0:
  218.7 137.6 reduce-scatter.1
